TPU v7x, 32 devices: a whole 2x2x4 slice. The times are simulated.
32 devices in a mesh: group: 2 (over x), seq: 8 (over z, y), head: 2 (over core).
Axes of the slice: x: 2, y: 2, z: 4, core: 2. Of those that a mesh axis runs over, the one named last changes fastest.
Arguments:
- queries: bfloat16 [4096, 8192], P(('group', 'seq', 'head')), parts along dimension 0, may hold values from -6 to 6
- keys: bfloat16 [4096, 1024], P(('group', 'seq', 'head')), parts along dimension 0, may hold values from -6 to 6
- values: bfloat16 [4096, 1024], P(('group', 'seq', 'head')), parts along dimension 0, may hold values from -6 to 6
- lengths: int32 [8], P('group'), parts along dimension 0, may hold values from 1 to 1024, 2048 in all
- assign: int32 [32], P('group'), parts along dimension 0, may hold values from 0 to 15, each once
Outputs:
- attended: bfloat16 [4096, 8192], P(('group', 'seq', 'head')), parts along dimension 0
There are 2 independent parts, one for each index of `group`. A program takes and returns all parts, laid end to end along the dimension named above; each array names one. Nothing has to cross between parts.
Inputs may be any that keep to these rules, and one draw needn't show every extreme that they name: 4 positive lengths summing to 2048, the largest exactly 1024. `assign`: each span index once.
All inputs are finite; a program needn't handle non-finite values.
Results may differ from a plain program's by a relative error of at most 0.004.
Values may be sent and summed in bfloat16 or wider, within the bound.
No kernel may reach another device: no remote copies, remote signals or barrier semaphores. Data moves between devices by JAX's collectives and lax.ppermute only.
A program may use at most 128 MiB of HBM per device.

v0:
```python
import functools
import math

import jax
import jax.numpy as jnp
from jax import lax
from jax.experimental import pallas as pl
from jax.experimental.pallas import tpu as pltpu
from jax.sharding import PartitionSpec as P


HEAD_SIZE = 128
AXES = ("seq", "head")
HIDDEN = -1e30
LANES = 128


def ring_of(mesh):
    count = mesh.shape["seq"]
    places = []
    for device in mesh.devices[0, :, 0].flat:
        places.append(tuple(getattr(device, "coords", ())))
    if len(set(places)) == count:
        varied = [axis for axis in range(len(places[0])) if len({place[axis] for place in places}) > 1]
        for narrow in varied:
            sides = sorted({place[narrow] for place in places})
            if len(varied) == 2 and len(sides) == 2:
                long = [axis for axis in varied if axis != narrow][0]
                up = sorted((p[long], i) for i, p in enumerate(places) if p[narrow] == sides[0])
                down = sorted((p[long], i) for i, p in enumerate(places) if p[narrow] == sides[1])
                return [i for _, i in up] + [i for _, i in reversed(down)]
    return list(range(count))


def longest(wide, most):
    _, depth = wide.shape
    place = lax.broadcasted_iota(jnp.int32, (depth, LANES), 0) // HEAD_SIZE
    member = (place == lax.broadcasted_iota(jnp.int32, (depth, LANES), 1)).astype(jnp.bfloat16)
    wide = wide.astype(jnp.float32)
    squares = jnp.dot((wide * wide).astype(jnp.bfloat16), member, preferred_element_type=jnp.float32)
    return squares if most is None else jnp.maximum(most, squares)


def shift_kernel(kv_heads, q_ref, k_ref, v_ref, info_ref, shift_out):
    wide = q_ref.shape[1] // kv_heads
    k_long = jnp.max(longest(k_ref[...], None))
    q_long = None
    for g in range(kv_heads):
        q_long = longest(q_ref[:, g * wide : (g + 1) * wide], q_long)
    product = jnp.full(shift_out.shape, jnp.max(q_long), jnp.float32) * k_long
    shift_out[...] = jnp.maximum(jnp.sqrt(product) * 1.02, 1e-3)


def shift_of(queries, keys, values, info, kv_heads):
    vmem = pl.BlockSpec(memory_space=pltpu.VMEM)
    return pl.pallas_call(
        functools.partial(shift_kernel, kv_heads),
        out_shape=jax.ShapeDtypeStruct((8, LANES), jnp.float32),
        in_specs=[vmem, vmem, vmem, pl.BlockSpec(memory_space=pltpu.SMEM)],
        out_specs=vmem,
        cost_estimate=pl.CostEstimate(
            flops=4 * queries.size * LANES, bytes_accessed=2 * queries.size, transcendentals=0
        ),
        compiler_params=pltpu.CompilerParams(vmem_limit_bytes=16 << 20),
        name="shift",
    )(queries, keys, values, info)


def attend_kernel(table, at, tail, part_of, blocks, spare, first, last, span, docs, kv_heads, query_group, *refs):
    info, q_ref = refs[:2]
    k_refs, v_refs = refs[2 : 2 + blocks], refs[2 + blocks : 2 + 2 * blocks]
    refs = refs[2 + 2 * blocks :]
    spare_k, spare_v = refs[:spare], refs[spare : 2 * spare]
    refs = refs[2 * spare :]
    shift_in = refs[0]
    refs = refs[1:]
    if last:
        least = refs[0]
        refs = refs[1:]
    if not first:
        acc_in, sum_in = refs[:2]
        refs = refs[2:]
    if last:
        out_ref = refs[0]
        refs = refs[1:]
    else:
        acc_out, sum_out = refs[:2]
        refs = refs[2:]
        if first:
            least = refs[0]
            refs = refs[1:]
    bias, values2 = refs[:2]
    wide = query_group * HEAD_SIZE
    if last:
        most_ref, all_k, all_v, sem, result, out_sem, places = refs[2:]

    mine = lax.axis_index("seq") * lax.axis_size("head") + lax.axis_index("head")

    def place_of(b):
        stored = jnp.int32(table[0][b])
        for device in range(1, len(table)):
            if table[device][b] != table[0][b]:
                stored = jnp.where(mine == device, table[device][b], stored)
        return info[docs + stored]

    own = place_of(0)
    factor = math.log2(math.e) / math.sqrt(HEAD_SIZE)
    place = [place_of(b) for b in at]
    ends = [info[0]]
    for d in range(1, docs):
        ends.append(ends[-1] + info[d])

    def begin_of(row):
        begin = jnp.zeros_like(row)
        for d in range(docs):
            begin = jnp.where(row >= ends[d], ends[d], begin)
        return begin

    def head_at(g, h):
        return pl.ds(pl.multiple_of((g * query_group + h) * HEAD_SIZE, HEAD_SIZE), HEAD_SIZE)

    shift = shift_in[0:1, :]
    low = begin_of(own * span + jnp.zeros((), jnp.int32))

    def sees(b):
        p = place_of(b)
        return ((p <= own) & (p * span + span > low)).astype(jnp.int32)

    seen = [sees(b) for b in at]
    if tail is not None:
        mine_now, swapped_now, final = tail
        n_mine = sum(sees(b) for b in mine_now)
        n_swapped = sum(sees(b) for b in swapped_now)
        n_final = sum(sees(b) for b in final)
        lone = (n_mine == 1) & (n_swapped == 1) & (n_final == 2)
        early = ((n_mine > 0) & jnp.logical_not(lone)).astype(jnp.int32)
        late = ((n_swapped == 1) & (n_final <= 1)).astype(jnp.int32)
        for i, b in enumerate(at):
            if last:
                seen[i] = seen[i] * (late if b in swapped_now else 1)
            elif len(at) == len(mine_now):
                seen[i] = seen[i] * early
            else:
                seen[i] = seen[i] * (1 - late) * (1 - early if b in mine_now else 1)
    before = []
    count = jnp.int32(0)
    for b in range(blocks):
        before.append(count)
        count = count + seen[b]

    def chosen(j):
        index, where = jnp.int32(0), jnp.int32(1 << 20)
        for b in range(blocks):
            hit = (seen[b] == 1) & (before[b] == j)
            index = jnp.where(hit, b, index)
            where = jnp.where(hit, place[b] * span, where)
        return index, where

    row = own * span + lax.broadcasted_iota(jnp.int32, (span, span), 0)
    begin = begin_of(row)
    minus = -factor * shift

    values2[:, HEAD_SIZE:] = jnp.ones((2 * span, HEAD_SIZE), jnp.bfloat16)
    if last:
        most_ref[...] = jnp.zeros((span, HEAD_SIZE), jnp.float32)

    def send_out(g):
        part = pl.ds(pl.multiple_of(g * wide, wide), wide)
        return pltpu.make_async_copy(result.at[:, part], out_ref.at[:, part], out_sem.at[g])

    low_g, high_g = (kv_heads * i // part_of[1] for i in (part_of[0], part_of[0] + 1))

    def two_blocks(pair, carry):
        picks = []
        for i in range(2):
            index, where = chosen(2 * pair + i)
            picks.append(index)
            column = where + lax.broadcasted_iota(jnp.int32, (span, span), 1)
            ok = (column >= begin) & (column <= row)
            bias[:, i * span : (i + 1) * span] = jnp.where(ok, minus, HIDDEN)

        def one_key_head(g, carry):
            at = pl.ds(pl.multiple_of(g * HEAD_SIZE, HEAD_SIZE), HEAD_SIZE)
            sides = []
            for sources in (k_refs, v_refs):
                tiles = []
                for i in range(2):
                    tile = sources[0][:, at]
                    for b in range(1, blocks):
                        tile = jnp.where(picks[i] == b, sources[b][:, at], tile)
                    tiles.append(tile)
                sides.append(jnp.concatenate(tiles, axis=0))
            sides[1] = jnp.concatenate([sides[1], values2[:, HEAD_SIZE:]], axis=1)
            heads = range(query_group)
            q_rows = jnp.concatenate([q_ref[:, head_at(g, h)] for h in heads], axis=0)
            scores = lax.dot_general(
                q_rows,
                sides[0],
                (((1,), (1,)), ((), ())),
                preferred_element_type=jnp.float32,
            )
            offset = jnp.concatenate([bias[...]] * query_group, axis=0)
            weights = jnp.exp2(scores * factor + offset).astype(jnp.bfloat16)
            product = jnp.dot(weights, sides[1], preferred_element_type=jnp.float32)
            if last:
                largest = most_ref[...]
            if first:
                smallest = least[...]
            for h in heads:
                here = head_at(g, h)
                part = product[h * span : (h + 1) * span, :HEAD_SIZE]
                total = product[h * span : (h + 1) * span, HEAD_SIZE:]
                if last:
                    part, total = part + acc_in[:, here], total + sum_in[:, here]
                    result[:, here] = (part / total).astype(result.dtype)
                    largest = jnp.maximum(largest, total)
                elif first:
                    smallest = jnp.minimum(smallest, total)
                    acc_out[:, here], sum_out[:, here] = part, total
                else:
                    acc_out[:, here] = acc_out[:, here] + part
                    sum_out[:, here] = sum_out[:, here] + total
            if first:
                least[...] = smallest
            if last:
                most_ref[...] = largest
                send_out(g).start()
            return carry

        lax.fori_loop(low_g, high_g, one_key_head, 0, unroll=True)
        return carry

    if first:
        least[...] = jnp.full(least.shape, 1.0, jnp.float32)
        two_blocks(0, 0)
    elif last:

        @pl.when(count > 0)
        def _():
            two_blocks(0, 0)

        @pl.when(count == 0)
        def _():
            def divide(g, carry):
                largest = most_ref[...]
                for h in range(query_group):
                    here = head_at(g, h)
                    total = sum_in[:, here]
                    result[:, here] = (acc_in[:, here] / total).astype(result.dtype)
                    largest = jnp.maximum(largest, total)
                most_ref[...] = largest
                send_out(g).start()
                return carry

            lax.fori_loop(0, kv_heads, divide, 0)
    else:
        lax.fori_loop(0, (count + 1) // 2, two_blocks, 0)

    if last:
        fair = (least[...] >= 2.0**-90) & (most_ref[...] <= 1.0)
        good = jnp.min(jnp.where(fair, 1.0, 0.0)) > 0.5
        for g in range(kv_heads):
            send_out(g).wait()

        @pl.when(jnp.logical_not(good))
        def _():
            for b in range(spare):
                places[b] = place_of(b)
            tall_row = own * span + lax.broadcasted_iota(jnp.int32, (span, span), 0)
            tall_begin = begin_of(tall_row)

            def one_key_head(g, carry):
                at = pl.ds(pl.multiple_of(g * HEAD_SIZE, HEAD_SIZE), HEAD_SIZE)
                for b in range(spare):
                    for source, target in ((spare_k[b], all_k), (spare_v[b], all_v)):
                        copy = pltpu.make_async_copy(
                            source.at[:, at], target.at[b * span : (b + 1) * span, :], sem
                        )
                        copy.start()
                        copy.wait()

                def one_head(h, carry):
                    here = head_at(g, h)

                    def one_block(b, state):
                        top, total, part = state
                        tall = pl.ds(pl.multiple_of(b * span, span), span)
                        column = places[b] * span + lax.broadcasted_iota(
                            jnp.int32, (span, span), 1
                        )
                        ok = (column >= tall_begin) & (column <= tall_row)
                        scores = lax.dot_general(
                            q_ref[:, here],
                            all_k[tall, :],
                            (((1,), (1,)), ((), ())),
                            preferred_element_type=jnp.float32,
                        )
                        scores = jnp.where(ok, scores * factor, HIDDEN)
                        newer = jnp.maximum(top, jnp.max(scores, axis=1, keepdims=True))
                        weights = jnp.where(ok, jnp.exp2(scores - newer), 0.0)
                        fade = jnp.exp2(top - newer)
                        total = total * fade + jnp.sum(weights, axis=1, keepdims=True)
                        part = part * fade + jnp.dot(
                            weights.astype(jnp.bfloat16),
                            all_v[tall, :],
                            preferred_element_type=jnp.float32,
                        )
                        return newer, total, part

                    start = (
                        jnp.full((span, 1), HIDDEN, jnp.float32),
                        jnp.zeros((span, 1), jnp.float32),
                        jnp.zeros((span, HEAD_SIZE), jnp.float32),
                    )
                    _, total, part = lax.fori_loop(0, spare, one_block, start)
                    result[:, here] = (part / total).astype(result.dtype)
                    return carry

                lax.fori_loop(0, query_group, one_head, 0)
                send_out(g).start()
                send_out(g).wait()
                return carry

            lax.fori_loop(0, kv_heads, one_key_head, 0)


def attend(table, at, tail, part_of, info, queries, keys, values, shift, state, every, docs, span, kv_heads):
    blocks = len(keys)
    first, last = state is None, every is not None
    spare = len(every[0]) if last else 0
    query_group = queries.shape[1] // (kv_heads * HEAD_SIZE)
    wide = jax.ShapeDtypeStruct(queries.shape, jnp.float32)
    vmem = pl.BlockSpec(memory_space=pltpu.VMEM)
    smem = pl.BlockSpec(memory_space=pltpu.SMEM)
    loose = pl.BlockSpec(memory_space=pl.ANY)
    inputs = [info, queries, *keys, *values]
    specs = [smem] + [vmem] * (1 + 2 * blocks)
    if last:
        inputs += [*every[0], *every[1]]
        specs += [loose] * (2 * spare)
    inputs += [shift] + ([] if first else [state[2]] * last + list(state[:2]))
    specs += [vmem] * (1 if first else 3 + last)
    aliases = {}
    if last:
        shapes, outs = jax.ShapeDtypeStruct(queries.shape, jnp.bfloat16), loose
    else:
        shapes, outs = (wide, wide), (vmem,) * 2
        if first:
            shapes += (jax.ShapeDtypeStruct((span, HEAD_SIZE), jnp.float32),)
            outs = (vmem,) * 3
        else:
            base = 3 + 2 * blocks
            aliases = {base: 0, base + 1: 1}
    scratch = [
        pltpu.VMEM((span, 2 * span), jnp.float32),
        pltpu.VMEM((2 * span, 2 * HEAD_SIZE), jnp.bfloat16),
    ]
    if last:
        scratch += [
            pltpu.VMEM((span, HEAD_SIZE), jnp.float32),
            pltpu.VMEM((span * spare, HEAD_SIZE), jnp.bfloat16),
            pltpu.VMEM((span * spare, HEAD_SIZE), jnp.bfloat16),
            pltpu.SemaphoreType.DMA,
            pltpu.VMEM(queries.shape, jnp.bfloat16),
            pltpu.SemaphoreType.DMA((kv_heads,)),
            pltpu.SMEM((spare,), jnp.int32),
        ]
    area = span * span * blocks * kv_heads * query_group
    result = pl.pallas_call(
        functools.partial(
            attend_kernel, table, at, tail, part_of, blocks, spare, first, last, span, docs, kv_heads, query_group
        ),
        out_shape=shapes,
        in_specs=specs,
        out_specs=outs,
        scratch_shapes=scratch,
        input_output_aliases=aliases,
        cost_estimate=pl.CostEstimate(
            flops=2 * area * HEAD_SIZE, bytes_accessed=4 * queries.size, transcendentals=area // 2
        ),
        compiler_params=pltpu.CompilerParams(vmem_limit_bytes=16 << 20),
        name="attend",
    )(*inputs)
    return result if first or last else (*result, state[2])


def solution(mesh):
    ring = ring_of(mesh)
    chips = len(ring)
    cores = mesh.shape["head"]
    spot = {seq: i for i, seq in enumerate(ring)}

    def along(step):
        return [
            (ring[i] * cores + c, ring[(i + step) % chips] * cores + c)
            for i in range(chips)
            for c in range(cores)
        ]

    def across(turn):
        return [
            (s * cores + c, s * cores + (c + turn) % cores)
            for s in range(chips)
            for c in range(cores)
        ]

    forward, backward = along(1), along(-1)

    def source(me, core, step, turn):
        seq = ring[(spot[me] - step) % chips]
        return seq * cores + (core - turn) % cores

    steps = list(range(1, (chips + 1) // 2))
    whole_order = [(0, t) for t in range(cores)]
    for s in steps:
        whole_order += [(d, t) for d in (s, -s) for t in range(cores)]
    if chips % 2 == 0:
        whole_order += [(chips // 2, t) for t in range(cores)]
    table = [
        [source(me, core, d, t) for d, t in whole_order] for me in range(chips) for core in range(cores)
    ]

    def local(queries, keys, values, lengths, assign):
        span = queries.shape[0]
        kv_heads = keys.shape[1] // HEAD_SIZE
        info = jnp.concatenate([lengths, assign])
        docs = lengths.shape[0]
        every = [[None] * len(table[0]), [None] * len(table[0])]

        def send(array, pairs):
            return lax.ppermute(array, AXES, pairs)

        def shared(array):
            return [array] + [send(array, across(t)) for t in range(1, cores)]

        def call(state, at, tail=None, part_of=(0, 1), last=False):
            keys, values = [every[0][b] for b in at], [every[1][b] for b in at]
            return attend(
                table,
                at,
                tail,
                part_of,
                info,
                queries,
                keys,
                values,
                shift,
                state,
                every if last else None,
                docs,
                span,
                kv_heads,
            )

        shift = shift_of(queries, keys, values, info, kv_heads)

        def arrived(begin, keys, values):
            every[0][begin : begin + len(keys)] = keys
            every[1][begin : begin + len(values)] = values
            return tuple(range(begin, begin + len(keys)))

        at = arrived(0, shared(keys), shared(values))
        state = call(None, at)
        kf = kb = keys
        vf = vb = values
        for s in steps:
            kf, kb = send(kf, forward), send(kb, backward)
            vf, vb = send(vf, forward), send(vb, backward)
            at = arrived(at[-1] + 1, shared(kf) + shared(kb), shared(vf) + shared(vb))
            if s < steps[-1]:
                state = call(state, at)
        s = steps[-1] + 1
        kf, vb = send(kf, forward), send(vb, backward)
        final = arrived(at[-1] + 1, shared(kf), shared(vb))
        mine_now = tuple(b for b in at if (b - at[0]) % cores == 0)
        swapped_now = tuple(b for b in at if b not in mine_now)
        tail = (mine_now, swapped_now, final)
        state = call(state, mine_now, tail)
        for i in (0, 1):
            state = call(state, at, tail, (i, 2))
        return call(state, swapped_now + final, tail, last=True)


    placed = P(("group", "seq", "head"), None)
    return jax.shard_map(
        local,
        mesh=mesh,
        in_specs=(placed, placed, placed, P("group"), P("group")),
        out_specs=placed,
        check_vma=False,
    )
```

profile of v0, /device:TPU:0, one launch (start us, length us, event | category | flops | bytes accessed | tf_op | source)
XLA Modules:
  0.0 451.3 jit_solution(17706920342146267916)
XLA Ops:
  0.0 0.5 collective-permute-start.20
  0.5 2.6 collective-permute-start
  3.1 2.0 collective-permute-start.10
  5.1 5.3 %collective-permute-done.refs_2_.refs_12_ = bf16[128,1024]{1,0:T(8,128)(2,1)S(1)} collective-permute-done((bf16[128,1024]{1,0:T(8,128)(2,1)}, bf16[128,1024]{1,0:T(8,128)(2,1)S(1)}, u32[]{:S(2)}, u32[]{:S(2)}) %collective-permute-start) | collective-permute-done | bytes 262176 | tf_op jit(solution)/shard_map/ppermute | solution.py:431
  10.4 2.1 collective-permute-done.4.refs_4_.refs_14_
  12.4 3.4 collective-permute-done.10.refs_6_.refs_28_
  15.8 1.8 collective-permute-start.1
  17.8 1.8 collective-permute-start.11
  19.9 5.1 %collective-permute-done.1.refs_2_.refs_16_ = bf16[128,1024]{1,0:T(8,128)(2,1)S(1)} collective-permute-done((bf16[128,1024]{1,0:T(8,128)(2,1)S(1)}, bf16[128,1024]{1,0:T(8,128)(2,1)S(1)}, u32[]{:S(2)}, u32[]{:S(2)}) %collective-permute-start.1) | collective-permute-done | bytes 262176 | tf_op jit(solution)/shard_map/ppermute | solution.py:431
  25.0 1.8 collective-permute-done.5.refs_4_.refs_18_
  26.8 3.4 collective-permute-done.11.refs_6_.refs_32_
  30.2 1.5 collective-permute-done.15.refs_8_.refs_34_
  32.1 1.6 collective-permute-start.2
  33.8 1.6 collective-permute-start.12
  35.3 0.4 collective-permute-start.6
  35.8 4.9 %collective-permute-done.16.refs_5_.refs_8_.refs_38_ = bf16[128,1024]{1,0:T(8,128)(2,1)S(1)} collective-permute-done((bf16[128,1024]{1,0:T(8,128)(2,1)S(1)}, bf16[128,1024]{1,0:T(8,128)(2,1)S(1)}, u32[]{:S(2)}, u32[]{:S(2)}) %collective-permute-start.16) | collective-permute-done | bytes 262176 | tf_op jit(solution)/shard_map/ppermute | solution.py:431
  40.7 0.5 collective-permute-start.18
  41.3 1.6 collective-permute-start.8
  42.9 0.7 pad_add_fusion.info_ref.refs_0_
  43.7 1.6 copy-done
  45.3 0.9 copy-done.1
  46.2 0.9 copy-done.3
  47.2 1.5 shift.1.refs_6_.refs_10_.refs_42_
  48.8 0.5 collective-permute-start.13
  49.3 3.0 attend.7
  52.4 0.6 attend.8
  53.0 0.5 collective-permute-start.19
  53.6 3.2 attend.9
  56.8 0.8 attend.10
  57.6 0.6 attend.11
  58.3 0.6 attend.12
  59.2 391.9 %attend.13 = bf16[128,8192]{1,0:T(8,128)(2,1)} custom-call(s32[20]{0:T(128)S(1)} %pad_add_fusion.info_ref.refs_0_, bf16[128,8192]{1,0:T(8,128)(2,1)S(1)} %copy-done, bf16[128,1024]{1,0:T(8,128)(2,1)S(1)} %collective-permute-done.3.refs_3_.refs_2_.refs_21_, bf16[128,1024]{1,0:T(8,128)(2,1)S(1)} %collective-permute-done.7.refs_5_.refs_3_.refs_23_, ...), custom_call_target="tpu_custom_call" | custom-call | flops 1073741824 | bytes 4194304 | tf_op jit(solution)/shard_map/attend/pallas_call | solution.py:369
  (45 shorter events, 1.7 us)
Async XLA Ops:
  0.0 5.1 %collective-permute-start.20 = (bf16[128,1024]{1,0:T(8,128)(2,1)}, bf16[128,1024]{1,0:T(8,128)(2,1)S(1)}, u32[]{:S(2)}, u32[]{:S(2)}) collective-permute-start(bf16[128,1024]{1,0:T(8,128)(2,1)} %refs_10_.1), channel_id=1, source_target_pairs={{0,1},{1,0},{2,3},{3,2},{4,5},{5,4},{6,7},{7,6},{8,9},{9,8},{10,11... | collective-permute-start | bytes 786440 | tf_op jit(solution)/shard_map/ppermute | solution.py:431
  0.5 9.9 %collective-permute-start = (bf16[128,1024]{1,0:T(8,128)(2,1)}, bf16[128,1024]{1,0:T(8,128)(2,1)S(1)}, u32[]{:S(2)}, u32[]{:S(2)}) collective-permute-start(bf16[128,1024]{1,0:T(8,128)(2,1)} %refs_10_.1), channel_id=1, source_target_pairs={{0,4},{1,5},{4,8},{5,9},{8,12},{9,13},{12,14},{13,15},{14,10},{15,... | collective-permute-start | bytes 786440 | tf_op jit(solution)/shard_map/ppermute | solution.py:431
  3.1 9.4 %collective-permute-start.4 = (bf16[128,1024]{1,0:T(8,128)(2,1)}, bf16[128,1024]{1,0:T(8,128)(2,1)S(1)}, u32[]{:S(2)}, u32[]{:S(2)}) collective-permute-start(bf16[128,1024]{1,0:T(8,128)(2,1)} %refs_10_.1), channel_id=1, source_target_pairs={{0,2},{1,3},{4,0},{5,1},{8,4},{9,5},{12,8},{13,9},{14,12},{15,13},... | collective-permute-start | bytes 786440 | tf_op jit(solution)/shard_map/ppermute | solution.py:431
  3.1 12.7 %collective-permute-start.10 = (bf16[128,1024]{1,0:T(8,128)(2,1)}, bf16[128,1024]{1,0:T(8,128)(2,1)S(1)}, u32[]{:S(2)}, u32[]{:S(2)}) collective-permute-start(bf16[128,1024]{1,0:T(8,128)(2,1)} %refs_26_.1), channel_id=1, source_target_pairs={{0,4},{1,5},{4,8},{5,9},{8,12},{9,13},{12,14},{13,15},{14,10},{15,... | collective-permute-start | bytes 786440 | tf_op jit(solution)/shard_map/ppermute | solution.py:431
  5.1 10.7 %collective-permute-start.25 = (bf16[128,1024]{1,0:T(8,128)(2,1)}, bf16[128,1024]{1,0:T(8,128)(2,1)S(1)}, u32[]{:S(2)}, u32[]{:S(2)}) collective-permute-start(bf16[128,1024]{1,0:T(8,128)(2,1)} %refs_26_.1), channel_id=1, source_target_pairs={{0,1},{1,0},{2,3},{3,2},{4,5},{5,4},{6,7},{7,6},{8,9},{9,8},{10,11... | collective-permute-start | bytes 786440 | tf_op jit(solution)/shard_map/ppermute | solution.py:431
  5.1 12.5 %collective-permute-start.14 = (bf16[128,1024]{1,0:T(8,128)(2,1)}, bf16[128,1024]{1,0:T(8,128)(2,1)S(1)}, u32[]{:S(2)}, u32[]{:S(2)}) collective-permute-start(bf16[128,1024]{1,0:T(8,128)(2,1)} %refs_26_.1), channel_id=1, source_target_pairs={{0,2},{1,3},{4,0},{5,1},{8,4},{9,5},{12,8},{13,9},{14,12},{15,13},... | collective-permute-start | bytes 786440 | tf_op jit(solution)/shard_map/ppermute | solution.py:431
  10.4 7.5 %collective-permute-start.21 = (bf16[128,1024]{1,0:T(8,128)(2,1)S(1)}, bf16[128,1024]{1,0:T(8,128)(2,1)S(1)}, u32[]{:S(2)}, u32[]{:S(2)}) collective-permute-start(bf16[128,1024]{1,0:T(8,128)(2,1)S(1)} %collective-permute-done.refs_2_.refs_12_), channel_id=1, source_target_pairs={{0,1},{1,0},{2,3},{3,2},{4,5},{5,4},{6,7},{7,6},{8,9},{9,8},{10,11... | collective-permute-start | bytes 786440 | tf_op jit(solution)/shard_map/ppermute | solution.py:431
  12.4 7.2 %collective-permute-start.22 = (bf16[128,1024]{1,0:T(8,128)(2,1)S(1)}, bf16[128,1024]{1,0:T(8,128)(2,1)S(1)}, u32[]{:S(2)}, u32[]{:S(2)}) collective-permute-start(bf16[128,1024]{1,0:T(8,128)(2,1)S(1)} %collective-permute-done.4.refs_4_.refs_14_), channel_id=1, source_target_pairs={{0,1},{1,0},{2,3},{3,2},{4,5},{5,4},{6,7},{7,6},{8,9},{9,8},{10,11... | collective-permute-start | bytes 786440 | tf_op jit(solution)/shard_map/ppermute | solution.py:431
  15.8 4.1 collective-permute-start.26
  15.8 9.2 %collective-permute-start.1 = (bf16[128,1024]{1,0:T(8,128)(2,1)S(1)}, bf16[128,1024]{1,0:T(8,128)(2,1)S(1)}, u32[]{:S(2)}, u32[]{:S(2)}) collective-permute-start(bf16[128,1024]{1,0:T(8,128)(2,1)S(1)} %collective-permute-done.refs_2_.refs_12_), channel_id=1, source_target_pairs={{0,4},{1,5},{4,8},{5,9},{8,12},{9,13},{12,14},{13,15},{14,10},{15,... | collective-permute-start | bytes 786440 | tf_op jit(solution)/shard_map/ppermute | solution.py:431
  17.6 9.2 %collective-permute-start.5 = (bf16[128,1024]{1,0:T(8,128)(2,1)S(1)}, bf16[128,1024]{1,0:T(8,128)(2,1)S(1)}, u32[]{:S(2)}, u32[]{:S(2)}) collective-permute-start(bf16[128,1024]{1,0:T(8,128)(2,1)S(1)} %collective-permute-done.4.refs_4_.refs_14_), channel_id=1, source_target_pairs={{0,2},{1,3},{4,0},{5,1},{8,4},{9,5},{12,8},{13,9},{14,12},{15,13},... | collective-permute-start | bytes 786440 | tf_op jit(solution)/shard_map/ppermute | solution.py:431
  17.8 12.3 %collective-permute-start.11 = (bf16[128,1024]{1,0:T(8,128)(2,1)S(1)}, bf16[128,1024]{1,0:T(8,128)(2,1)S(1)}, u32[]{:S(2)}, u32[]{:S(2)}) collective-permute-start(bf16[128,1024]{1,0:T(8,128)(2,1)S(1)} %collective-permute-done.10.refs_6_.refs_28_), channel_id=1, source_target_pairs={{0,4},{1,5},{4,8},{5,9},{8,12},{9,13},{12,14},{13,15},{14,10},{15,... | collective-permute-start | bytes 786440 | tf_op jit(solution)/shard_map/ppermute | solution.py:431
  19.6 12.0 %collective-permute-start.15 = (bf16[128,1024]{1,0:T(8,128)(2,1)S(1)}, bf16[128,1024]{1,0:T(8,128)(2,1)S(1)}, u32[]{:S(2)}, u32[]{:S(2)}) collective-permute-start(bf16[128,1024]{1,0:T(8,128)(2,1)S(1)} %collective-permute-done.14.refs_8_.refs_30_), channel_id=1, source_target_pairs={{0,2},{1,3},{4,0},{5,1},{8,4},{9,5},{12,8},{13,9},{14,12},{15,13},... | collective-permute-start | bytes 786440 | tf_op jit(solution)/shard_map/ppermute | solution.py:431
  19.9 12.1 %collective-permute-start.27 = (bf16[128,1024]{1,0:T(8,128)(2,1)S(1)}, bf16[128,1024]{1,0:T(8,128)(2,1)S(1)}, u32[]{:S(2)}, u32[]{:S(2)}) collective-permute-start(bf16[128,1024]{1,0:T(8,128)(2,1)S(1)} %collective-permute-done.14.refs_8_.refs_30_), channel_id=1, source_target_pairs={{0,1},{1,0},{2,3},{3,2},{4,5},{5,4},{6,7},{7,6},{8,9},{9,8},{10,11... | collective-permute-start | bytes 786440 | tf_op jit(solution)/shard_map/ppermute | solution.py:431
  25.0 7.1 %collective-permute-start.23 = (bf16[128,1024]{1,0:T(8,128)(2,1)S(1)}, bf16[128,1024]{1,0:T(8,128)(2,1)S(1)}, u32[]{:S(2)}, u32[]{:S(2)}) collective-permute-start(bf16[128,1024]{1,0:T(8,128)(2,1)S(1)} %collective-permute-done.1.refs_2_.refs_16_), channel_id=1, source_target_pairs={{0,1},{1,0},{2,3},{3,2},{4,5},{5,4},{6,7},{7,6},{8,9},{9,8},{10,11... | collective-permute-start | bytes 786440 | tf_op jit(solution)/shard_map/ppermute | solution.py:431
  26.8 7.0 %collective-permute-start.24 = (bf16[128,1024]{1,0:T(8,128)(2,1)S(1)}, bf16[128,1024]{1,0:T(8,128)(2,1)S(1)}, u32[]{:S(2)}, u32[]{:S(2)}) collective-permute-start(bf16[128,1024]{1,0:T(8,128)(2,1)S(1)} %collective-permute-done.5.refs_4_.refs_18_), channel_id=1, source_target_pairs={{0,1},{1,0},{2,3},{3,2},{4,5},{5,4},{6,7},{7,6},{8,9},{9,8},{10,11... | collective-permute-start | bytes 786440 | tf_op jit(solution)/shard_map/ppermute | solution.py:431
  30.1 5.2 %collective-permute-start.28 = (bf16[128,1024]{1,0:T(8,128)(2,1)S(1)}, bf16[128,1024]{1,0:T(8,128)(2,1)S(1)}, u32[]{:S(2)}, u32[]{:S(2)}) collective-permute-start(bf16[128,1024]{1,0:T(8,128)(2,1)S(1)} %collective-permute-done.11.refs_6_.refs_32_), channel_id=1, source_target_pairs={{0,1},{1,0},{2,3},{3,2},{4,5},{5,4},{6,7},{7,6},{8,9},{9,8},{10,11... | collective-permute-start | bytes 786440 | tf_op jit(solution)/shard_map/ppermute | solution.py:431
  31.7 9.0 %collective-permute-start.16 = (bf16[128,1024]{1,0:T(8,128)(2,1)S(1)}, bf16[128,1024]{1,0:T(8,128)(2,1)S(1)}, u32[]{:S(2)}, u32[]{:S(2)}) collective-permute-start(bf16[128,1024]{1,0:T(8,128)(2,1)S(1)} %collective-permute-done.15.refs_8_.refs_34_), channel_id=1, source_target_pairs={{0,2},{1,3},{4,0},{5,1},{8,4},{9,5},{12,8},{13,9},{14,12},{15,13},... | collective-permute-start | bytes 786440 | tf_op jit(solution)/shard_map/ppermute | solution.py:431
  32.0 8.7 %collective-permute-start.29 = (bf16[128,1024]{1,0:T(8,128)(2,1)S(1)}, bf16[128,1024]{1,0:T(8,128)(2,1)S(1)}, u32[]{:S(2)}, u32[]{:S(2)}) collective-permute-start(bf16[128,1024]{1,0:T(8,128)(2,1)S(1)} %collective-permute-done.15.refs_8_.refs_34_), channel_id=1, source_target_pairs={{0,1},{1,0},{2,3},{3,2},{4,5},{5,4},{6,7},{7,6},{8,9},{9,8},{10,11... | collective-permute-start | bytes 786440 | tf_op jit(solution)/shard_map/ppermute | solution.py:431
  32.1 9.2 %collective-permute-start.2 = (bf16[128,1024]{1,0:T(8,128)(2,1)S(1)}, bf16[128,1024]{1,0:T(8,128)(2,1)S(1)}, u32[]{:S(2)}, u32[]{:S(2)}) collective-permute-start(bf16[128,1024]{1,0:T(8,128)(2,1)S(1)} %collective-permute-done.1.refs_2_.refs_16_), channel_id=1, source_target_pairs={{0,4},{1,5},{4,8},{5,9},{8,12},{9,13},{12,14},{13,15},{14,10},{15,... | collective-permute-start | bytes 786440 | tf_op jit(solution)/shard_map/ppermute | solution.py:431
  33.8 14.9 %collective-permute-start.12 = (bf16[128,1024]{1,0:T(8,128)(2,1)S(1)}, bf16[128,1024]{1,0:T(8,128)(2,1)S(1)}, u32[]{:S(2)}, u32[]{:S(2)}) collective-permute-start(bf16[128,1024]{1,0:T(8,128)(2,1)S(1)} %collective-permute-done.11.refs_6_.refs_32_), channel_id=1, source_target_pairs={{0,4},{1,5},{4,8},{5,9},{8,12},{9,13},{12,14},{13,15},{14,10},{15,... | collective-permute-start | bytes 786440 | tf_op jit(solution)/shard_map/ppermute | solution.py:431
  35.3 13.4 %collective-permute-start.6 = (bf16[128,1024]{1,0:T(8,128)(2,1)S(1)}, bf16[128,1024]{1,0:T(8,128)(2,1)S(1)}, u32[]{:S(2)}, u32[]{:S(2)}) collective-permute-start(bf16[128,1024]{1,0:T(8,128)(2,1)S(1)} %collective-permute-done.5.refs_4_.refs_18_), channel_id=1, source_target_pairs={{0,2},{1,3},{4,0},{5,1},{8,4},{9,5},{12,8},{13,9},{14,12},{15,13},... | collective-permute-start | bytes 786440 | tf_op jit(solution)/shard_map/ppermute | solution.py:431
  40.7 8.6 %collective-permute-start.17 = (bf16[128,1024]{1,0:T(8,128)(2,1)S(1)}, bf16[128,1024]{1,0:T(8,128)(2,1)S(1)}, u32[]{:S(2)}, u32[]{:S(2)}) collective-permute-start(bf16[128,1024]{1,0:T(8,128)(2,1)S(1)} %collective-permute-done.16.refs_5_.refs_8_.refs_38_), channel_id=1, source_target_pairs={{0,1},{1,0},{2,3},{3,2},{4,5},{5,4},{6,7},{7,6},{8,9},{9,8},{10,11... | collective-permute-start | bytes 786440 | tf_op jit(solution)/shard_map/ppermute | solution.py:431
  40.7 12.3 %collective-permute-start.18 = (bf16[128,1024]{1,0:T(8,128)(2,1)S(1)}, bf16[128,1024]{1,0:T(8,128)(2,1)S(1)}, u32[]{:S(2)}, u32[]{:S(2)}) collective-permute-start(bf16[128,1024]{1,0:T(8,128)(2,1)S(1)} %collective-permute-done.16.refs_5_.refs_8_.refs_38_), channel_id=1, source_target_pairs={{0,2},{1,3},{4,0},{5,1},{8,4},{9,5},{12,8},{13,9},{14,12},{15,13},... | collective-permute-start | bytes 786440 | tf_op jit(solution)/shard_map/ppermute | solution.py:431
  41.3 12.2 %collective-permute-start.8 = (bf16[128,1024]{1,0:T(8,128)(2,1)S(1)}, bf16[128,1024]{1,0:T(8,128)(2,1)S(1)}, u32[]{:S(2)}, u32[]{:S(2)}) collective-permute-start(bf16[128,1024]{1,0:T(8,128)(2,1)S(1)} %collective-permute-done.2.refs_2_.refs_20_), channel_id=1, source_target_pairs={{0,4},{1,5},{4,8},{5,9},{8,12},{9,13},{12,14},{13,15},{14,10},{15,... | collective-permute-start | bytes 786440 | tf_op jit(solution)/shard_map/ppermute | solution.py:431
  43.7 1.6 copy-start
  48.7 8.9 %collective-permute-start.3 = (bf16[128,1024]{1,0:T(8,128)(2,1)S(1)}, bf16[128,1024]{1,0:T(8,128)(2,1)S(1)}, u32[]{:S(2)}, u32[]{:S(2)}) collective-permute-start(bf16[128,1024]{1,0:T(8,128)(2,1)S(1)} %collective-permute-done.2.refs_2_.refs_20_), channel_id=1, source_target_pairs={{0,1},{1,0},{2,3},{3,2},{4,5},{5,4},{6,7},{7,6},{8,9},{9,8},{10,11... | collective-permute-start | bytes 786440 | tf_op jit(solution)/shard_map/ppermute | solution.py:431
  48.8 8.8 %collective-permute-start.13 = (bf16[128,1024]{1,0:T(8,128)(2,1)S(1)}, bf16[128,1024]{1,0:T(8,128)(2,1)S(1)}, u32[]{:S(2)}, u32[]{:S(2)}) collective-permute-start(bf16[128,1024]{1,0:T(8,128)(2,1)S(1)} %collective-permute-done.12.refs_4_.refs_6_.refs_36_), channel_id=1, source_target_pairs={{0,1},{1,0},{2,3},{3,2},{4,5},{5,4},{6,7},{7,6},{8,9},{9,8},{10,11... | collective-permute-start | bytes 786440 | tf_op jit(solution)/shard_map/ppermute | solution.py:431
  49.2 8.4 %collective-permute-start.7 = (bf16[128,1024]{1,0:T(8,128)(2,1)S(1)}, bf16[128,1024]{1,0:T(8,128)(2,1)S(1)}, u32[]{:S(2)}, u32[]{:S(2)}) collective-permute-start(bf16[128,1024]{1,0:T(8,128)(2,1)S(1)} %collective-permute-done.6.refs_3_.refs_4_.refs_22_), channel_id=1, source_target_pairs={{0,1},{1,0},{2,3},{3,2},{4,5},{5,4},{6,7},{7,6},{8,9},{9,8},{10,11... | collective-permute-start | bytes 786440 | tf_op jit(solution)/shard_map/ppermute | solution.py:431
  53.0 5.9 %collective-permute-start.19 = (bf16[128,1024]{1,0:T(8,128)(2,1)S(1)}, bf16[128,1024]{1,0:T(8,128)(2,1)S(1)}, u32[]{:S(2)}, u32[]{:S(2)}) collective-permute-start(bf16[128,1024]{1,0:T(8,128)(2,1)S(1)} %collective-permute-done.18.refs_8_.refs_40_), channel_id=1, source_target_pairs={{0,1},{1,0},{2,3},{3,2},{4,5},{5,4},{6,7},{7,6},{8,9},{9,8},{10,11... | collective-permute-start | bytes 786440 | tf_op jit(solution)/shard_map/ppermute | solution.py:431
  53.5 5.4 %collective-permute-start.9 = (bf16[128,1024]{1,0:T(8,128)(2,1)S(1)}, bf16[128,1024]{1,0:T(8,128)(2,1)S(1)}, u32[]{:S(2)}, u32[]{:S(2)}) collective-permute-start(bf16[128,1024]{1,0:T(8,128)(2,1)S(1)} %collective-permute-done.8.refs_4_.refs_24_), channel_id=1, source_target_pairs={{0,1},{1,0},{2,3},{3,2},{4,5},{5,4},{6,7},{7,6},{8,9},{9,8},{10,11... | collective-permute-start | bytes 786440 | tf_op jit(solution)/shard_map/ppermute | solution.py:431
  58.3 1.0 copy-start.2
  (2 other events, 1.9 us)
where the time goes:
time: 459 us; the launch traced here: 451 us
  Pallas kernels  402 us (88%)
  waiting for transfers between devices  27.6 us (6%)
  starting transfers between devices  16.6 us (4%)
    pallas_call x7, Pallas kernels, attend(): pl.pallas_call(functools.partial(attend_kernel, table, at, tail, part_of,...  401 us
    ppermute x30, waiting for transfers between devices, send(): return lax.ppermute(array, AXES, pairs)  27.6 us
    ppermute x30, starting transfers between devices, send(): return lax.ppermute(array, AXES, pairs)  16.6 us
  transfers between devices with their start and end apart: 30, of which 9 were waited for; matrix products, arithmetic and copies ran while one was open for 0% of the time, Pallas kernels for 2%

commit v1 on v0

--- a/solution.py
+++ b/solution.py
@@ -132,9 +132,9 @@
         n_mine = sum(sees(b) for b in mine_now)
         n_swapped = sum(sees(b) for b in swapped_now)
         n_final = sum(sees(b) for b in final)
-        lone = (n_mine == 1) & (n_swapped == 1) & (n_final == 2)
-        early = ((n_mine > 0) & jnp.logical_not(lone)).astype(jnp.int32)
-        late = ((n_swapped == 1) & (n_final <= 1)).astype(jnp.int32)
+        early = ((n_mine == 2) | ((n_mine == 1) & (n_swapped != 1))).astype(jnp.int32)
+        rest = (1 - early) * n_mine + n_swapped
+        late = ((rest == 1) & (n_final == 1)).astype(jnp.int32)
         for i, b in enumerate(at):
             if last:
                 seen[i] = seen[i] * (late if b in swapped_now else 1)
@@ -468,7 +468,8 @@
             vf, vb = send(vf, forward), send(vb, backward)
             at = arrived(at[-1] + 1, shared(kf) + shared(kb), shared(vf) + shared(vb))
             if s < steps[-1]:
-                state = call(state, at)
+                for i in (0, 1):
+                    state = call(state, at, None, (i, 2))
         s = steps[-1] + 1
         kf, vb = send(kf, forward), send(vb, backward)
         final = arrived(at[-1] + 1, shared(kf), shared(vb))

time: 459 us -> 462 us (level)
    pallas_call x7 -> x9, Pallas kernels: 401 us -> 402 us  [attend(): pl.pallas_call(functools.partial(attend_kernel, table, at, tail, part_of,...]
  transfers between devices with their start and end apart: 30 -> 30, of which waited for: 9 -> 10; matrix products, arithmetic and copies ran while one was open for 0% -> 0% of each run, Pallas kernels for 2% -> 3%
where the time goes in v1:
time: 462 us; the launch traced here: 455 us
  Pallas kernels  404 us (87%)
  waiting for transfers between devices  30.3 us (7%)
  starting transfers between devices  16.3 us (4%)
    pallas_call x9, Pallas kernels, attend(): pl.pallas_call(functools.partial(attend_kernel, table, at, tail, part_of,...  402 us
    ppermute x30, waiting for transfers between devices, send(): return lax.ppermute(array, AXES, pairs)  30.3 us
    ppermute x30, starting transfers between devices, send(): return lax.ppermute(array, AXES, pairs)  16.3 us
  transfers between devices with their start and end apart: 30, of which 10 were waited for; matrix products, arithmetic and copies ran while one was open for 0% of the time, Pallas kernels for 3%

profile of v1, /device:TPU:0, one launch (start us, length us, event | category | flops | bytes accessed | tf_op | source)
XLA Modules:
  0.0 455.4 jit_solution(535382245816760817)
XLA Ops:
  0.0 0.5 collective-permute-start.20
  0.5 2.6 collective-permute-start
  3.1 2.0 collective-permute-start.10
  5.1 5.3 %collective-permute-done.refs_2_.refs_12_ = bf16[128,1024]{1,0:T(8,128)(2,1)S(1)} collective-permute-done((bf16[128,1024]{1,0:T(8,128)(2,1)}, bf16[128,1024]{1,0:T(8,128)(2,1)S(1)}, u32[]{:S(2)}, u32[]{:S(2)}) %collective-permute-start) | collective-permute-done | bytes 262176 | tf_op jit(solution)/shard_map/ppermute | solution.py:431
  10.4 2.1 collective-permute-done.4.refs_4_.refs_14_
  12.4 3.4 collective-permute-done.10.refs_6_.refs_28_
  15.8 1.8 collective-permute-start.1
  17.8 1.8 collective-permute-start.11
  19.9 5.1 %collective-permute-done.1.refs_2_.refs_16_ = bf16[128,1024]{1,0:T(8,128)(2,1)S(1)} collective-permute-done((bf16[128,1024]{1,0:T(8,128)(2,1)S(1)}, bf16[128,1024]{1,0:T(8,128)(2,1)S(1)}, u32[]{:S(2)}, u32[]{:S(2)}) %collective-permute-start.1) | collective-permute-done | bytes 262176 | tf_op jit(solution)/shard_map/ppermute | solution.py:431
  25.0 1.8 collective-permute-done.5.refs_4_.refs_18_
  26.8 3.4 collective-permute-done.11.refs_6_.refs_32_
  30.2 1.5 collective-permute-done.15.refs_8_.refs_34_
  32.1 1.6 collective-permute-start.2
  33.8 1.6 collective-permute-start.12
  35.8 4.9 %collective-permute-done.16.refs_5_.refs_8_.refs_38_ = bf16[128,1024]{1,0:T(8,128)(2,1)S(1)} collective-permute-done((bf16[128,1024]{1,0:T(8,128)(2,1)S(1)}, bf16[128,1024]{1,0:T(8,128)(2,1)S(1)}, u32[]{:S(2)}, u32[]{:S(2)}) %collective-permute-start.16) | collective-permute-done | bytes 262176 | tf_op jit(solution)/shard_map/ppermute | solution.py:431
  40.7 0.7 pad_add_fusion.info_ref.refs_0_
  41.4 1.6 copy-done
  43.0 0.9 copy-done.1
  44.0 0.9 copy-done.3
  44.9 1.5 shift.1.refs_6_.refs_10_.refs_42_
  46.4 3.0 attend.9
  49.4 0.5 collective-permute-start.18
  50.0 1.6 collective-permute-start.8
  51.5 0.6 attend.10
  52.8 0.6 attend.11
  53.4 2.0 attend.12
  55.5 2.7 collective-permute-done.18.refs_8_.refs_40_
  58.7 2.2 attend.13
  60.9 0.6 attend.14
  61.6 0.6 attend.15
  62.2 0.6 attend.16
  63.2 392.1 %attend.17 = bf16[128,8192]{1,0:T(8,128)(2,1)} custom-call(s32[20]{0:T(128)S(1)} %pad_add_fusion.info_ref.refs_0_, bf16[128,8192]{1,0:T(8,128)(2,1)S(1)} %copy-done, bf16[128,1024]{1,0:T(8,128)(2,1)S(1)} %collective-permute-done.3.refs_3_.refs_2_.refs_21_, bf16[128,1024]{1,0:T(8,128)(2,1)S(1)} %collective-permute-done.7.refs_5_.refs_3_.refs_23_, ...), custom_call_target="tpu_custom_call" | custom-call | flops 1073741824 | bytes 4194304 | tf_op jit(solution)/shard_map/attend/pallas_call | solution.py:369
  (47 shorter events, 2.9 us)
Async XLA Ops:
  0.0 5.1 %collective-permute-start.20 = (bf16[128,1024]{1,0:T(8,128)(2,1)}, bf16[128,1024]{1,0:T(8,128)(2,1)S(1)}, u32[]{:S(2)}, u32[]{:S(2)}) collective-permute-start(bf16[128,1024]{1,0:T(8,128)(2,1)} %refs_10_.1), channel_id=1, source_target_pairs={{0,1},{1,0},{2,3},{3,2},{4,5},{5,4},{6,7},{7,6},{8,9},{9,8},{10,11... | collective-permute-start | bytes 786440 | tf_op jit(solution)/shard_map/ppermute | solution.py:431
  0.5 9.9 %collective-permute-start = (bf16[128,1024]{1,0:T(8,128)(2,1)}, bf16[128,1024]{1,0:T(8,128)(2,1)S(1)}, u32[]{:S(2)}, u32[]{:S(2)}) collective-permute-start(bf16[128,1024]{1,0:T(8,128)(2,1)} %refs_10_.1), channel_id=1, source_target_pairs={{0,4},{1,5},{4,8},{5,9},{8,12},{9,13},{12,14},{13,15},{14,10},{15,... | collective-permute-start | bytes 786440 | tf_op jit(solution)/shard_map/ppermute | solution.py:431
  3.1 9.4 %collective-permute-start.4 = (bf16[128,1024]{1,0:T(8,128)(2,1)}, bf16[128,1024]{1,0:T(8,128)(2,1)S(1)}, u32[]{:S(2)}, u32[]{:S(2)}) collective-permute-start(bf16[128,1024]{1,0:T(8,128)(2,1)} %refs_10_.1), channel_id=1, source_target_pairs={{0,2},{1,3},{4,0},{5,1},{8,4},{9,5},{12,8},{13,9},{14,12},{15,13},... | collective-permute-start | bytes 786440 | tf_op jit(solution)/shard_map/ppermute | solution.py:431
  3.1 12.7 %collective-permute-start.10 = (bf16[128,1024]{1,0:T(8,128)(2,1)}, bf16[128,1024]{1,0:T(8,128)(2,1)S(1)}, u32[]{:S(2)}, u32[]{:S(2)}) collective-permute-start(bf16[128,1024]{1,0:T(8,128)(2,1)} %refs_26_.1), channel_id=1, source_target_pairs={{0,4},{1,5},{4,8},{5,9},{8,12},{9,13},{12,14},{13,15},{14,10},{15,... | collective-permute-start | bytes 786440 | tf_op jit(solution)/shard_map/ppermute | solution.py:431
  5.1 10.7 %collective-permute-start.25 = (bf16[128,1024]{1,0:T(8,128)(2,1)}, bf16[128,1024]{1,0:T(8,128)(2,1)S(1)}, u32[]{:S(2)}, u32[]{:S(2)}) collective-permute-start(bf16[128,1024]{1,0:T(8,128)(2,1)} %refs_26_.1), channel_id=1, source_target_pairs={{0,1},{1,0},{2,3},{3,2},{4,5},{5,4},{6,7},{7,6},{8,9},{9,8},{10,11... | collective-permute-start | bytes 786440 | tf_op jit(solution)/shard_map/ppermute | solution.py:431
  5.1 12.5 %collective-permute-start.14 = (bf16[128,1024]{1,0:T(8,128)(2,1)}, bf16[128,1024]{1,0:T(8,128)(2,1)S(1)}, u32[]{:S(2)}, u32[]{:S(2)}) collective-permute-start(bf16[128,1024]{1,0:T(8,128)(2,1)} %refs_26_.1), channel_id=1, source_target_pairs={{0,2},{1,3},{4,0},{5,1},{8,4},{9,5},{12,8},{13,9},{14,12},{15,13},... | collective-permute-start | bytes 786440 | tf_op jit(solution)/shard_map/ppermute | solution.py:431
  10.4 7.5 %collective-permute-start.21 = (bf16[128,1024]{1,0:T(8,128)(2,1)S(1)}, bf16[128,1024]{1,0:T(8,128)(2,1)S(1)}, u32[]{:S(2)}, u32[]{:S(2)}) collective-permute-start(bf16[128,1024]{1,0:T(8,128)(2,1)S(1)} %collective-permute-done.refs_2_.refs_12_), channel_id=1, source_target_pairs={{0,1},{1,0},{2,3},{3,2},{4,5},{5,4},{6,7},{7,6},{8,9},{9,8},{10,11... | collective-permute-start | bytes 786440 | tf_op jit(solution)/shard_map/ppermute | solution.py:431
  12.4 7.2 %collective-permute-start.22 = (bf16[128,1024]{1,0:T(8,128)(2,1)S(1)}, bf16[128,1024]{1,0:T(8,128)(2,1)S(1)}, u32[]{:S(2)}, u32[]{:S(2)}) collective-permute-start(bf16[128,1024]{1,0:T(8,128)(2,1)S(1)} %collective-permute-done.4.refs_4_.refs_14_), channel_id=1, source_target_pairs={{0,1},{1,0},{2,3},{3,2},{4,5},{5,4},{6,7},{7,6},{8,9},{9,8},{10,11... | collective-permute-start | bytes 786440 | tf_op jit(solution)/shard_map/ppermute | solution.py:431
  15.8 4.1 collective-permute-start.26
  15.8 9.2 %collective-permute-start.1 = (bf16[128,1024]{1,0:T(8,128)(2,1)S(1)}, bf16[128,1024]{1,0:T(8,128)(2,1)S(1)}, u32[]{:S(2)}, u32[]{:S(2)}) collective-permute-start(bf16[128,1024]{1,0:T(8,128)(2,1)S(1)} %collective-permute-done.refs_2_.refs_12_), channel_id=1, source_target_pairs={{0,4},{1,5},{4,8},{5,9},{8,12},{9,13},{12,14},{13,15},{14,10},{15,... | collective-permute-start | bytes 786440 | tf_op jit(solution)/shard_map/ppermute | solution.py:431
  17.6 9.2 %collective-permute-start.5 = (bf16[128,1024]{1,0:T(8,128)(2,1)S(1)}, bf16[128,1024]{1,0:T(8,128)(2,1)S(1)}, u32[]{:S(2)}, u32[]{:S(2)}) collective-permute-start(bf16[128,1024]{1,0:T(8,128)(2,1)S(1)} %collective-permute-done.4.refs_4_.refs_14_), channel_id=1, source_target_pairs={{0,2},{1,3},{4,0},{5,1},{8,4},{9,5},{12,8},{13,9},{14,12},{15,13},... | collective-permute-start | bytes 786440 | tf_op jit(solution)/shard_map/ppermute | solution.py:431
  17.8 12.3 %collective-permute-start.11 = (bf16[128,1024]{1,0:T(8,128)(2,1)S(1)}, bf16[128,1024]{1,0:T(8,128)(2,1)S(1)}, u32[]{:S(2)}, u32[]{:S(2)}) collective-permute-start(bf16[128,1024]{1,0:T(8,128)(2,1)S(1)} %collective-permute-done.10.refs_6_.refs_28_), channel_id=1, source_target_pairs={{0,4},{1,5},{4,8},{5,9},{8,12},{9,13},{12,14},{13,15},{14,10},{15,... | collective-permute-start | bytes 786440 | tf_op jit(solution)/shard_map/ppermute | solution.py:431
  19.6 12.0 %collective-permute-start.15 = (bf16[128,1024]{1,0:T(8,128)(2,1)S(1)}, bf16[128,1024]{1,0:T(8,128)(2,1)S(1)}, u32[]{:S(2)}, u32[]{:S(2)}) collective-permute-start(bf16[128,1024]{1,0:T(8,128)(2,1)S(1)} %collective-permute-done.14.refs_8_.refs_30_), channel_id=1, source_target_pairs={{0,2},{1,3},{4,0},{5,1},{8,4},{9,5},{12,8},{13,9},{14,12},{15,13},... | collective-permute-start | bytes 786440 | tf_op jit(solution)/shard_map/ppermute | solution.py:431
  19.9 12.1 %collective-permute-start.27 = (bf16[128,1024]{1,0:T(8,128)(2,1)S(1)}, bf16[128,1024]{1,0:T(8,128)(2,1)S(1)}, u32[]{:S(2)}, u32[]{:S(2)}) collective-permute-start(bf16[128,1024]{1,0:T(8,128)(2,1)S(1)} %collective-permute-done.14.refs_8_.refs_30_), channel_id=1, source_target_pairs={{0,1},{1,0},{2,3},{3,2},{4,5},{5,4},{6,7},{7,6},{8,9},{9,8},{10,11... | collective-permute-start | bytes 786440 | tf_op jit(solution)/shard_map/ppermute | solution.py:431
  25.0 7.1 %collective-permute-start.23 = (bf16[128,1024]{1,0:T(8,128)(2,1)S(1)}, bf16[128,1024]{1,0:T(8,128)(2,1)S(1)}, u32[]{:S(2)}, u32[]{:S(2)}) collective-permute-start(bf16[128,1024]{1,0:T(8,128)(2,1)S(1)} %collective-permute-done.1.refs_2_.refs_16_), channel_id=1, source_target_pairs={{0,1},{1,0},{2,3},{3,2},{4,5},{5,4},{6,7},{7,6},{8,9},{9,8},{10,11... | collective-permute-start | bytes 786440 | tf_op jit(solution)/shard_map/ppermute | solution.py:431
  26.8 7.0 %collective-permute-start.24 = (bf16[128,1024]{1,0:T(8,128)(2,1)S(1)}, bf16[128,1024]{1,0:T(8,128)(2,1)S(1)}, u32[]{:S(2)}, u32[]{:S(2)}) collective-permute-start(bf16[128,1024]{1,0:T(8,128)(2,1)S(1)} %collective-permute-done.5.refs_4_.refs_18_), channel_id=1, source_target_pairs={{0,1},{1,0},{2,3},{3,2},{4,5},{5,4},{6,7},{7,6},{8,9},{9,8},{10,11... | collective-permute-start | bytes 786440 | tf_op jit(solution)/shard_map/ppermute | solution.py:431
  30.1 5.2 %collective-permute-start.28 = (bf16[128,1024]{1,0:T(8,128)(2,1)S(1)}, bf16[128,1024]{1,0:T(8,128)(2,1)S(1)}, u32[]{:S(2)}, u32[]{:S(2)}) collective-permute-start(bf16[128,1024]{1,0:T(8,128)(2,1)S(1)} %collective-permute-done.11.refs_6_.refs_32_), channel_id=1, source_target_pairs={{0,1},{1,0},{2,3},{3,2},{4,5},{5,4},{6,7},{7,6},{8,9},{9,8},{10,11... | collective-permute-start | bytes 786440 | tf_op jit(solution)/shard_map/ppermute | solution.py:431
  31.7 9.0 %collective-permute-start.16 = (bf16[128,1024]{1,0:T(8,128)(2,1)S(1)}, bf16[128,1024]{1,0:T(8,128)(2,1)S(1)}, u32[]{:S(2)}, u32[]{:S(2)}) collective-permute-start(bf16[128,1024]{1,0:T(8,128)(2,1)S(1)} %collective-permute-done.15.refs_8_.refs_34_), channel_id=1, source_target_pairs={{0,2},{1,3},{4,0},{5,1},{8,4},{9,5},{12,8},{13,9},{14,12},{15,13},... | collective-permute-start | bytes 786440 | tf_op jit(solution)/shard_map/ppermute | solution.py:431
  32.0 17.5 %collective-permute-start.29 = (bf16[128,1024]{1,0:T(8,128)(2,1)S(1)}, bf16[128,1024]{1,0:T(8,128)(2,1)S(1)}, u32[]{:S(2)}, u32[]{:S(2)}) collective-permute-start(bf16[128,1024]{1,0:T(8,128)(2,1)S(1)} %collective-permute-done.15.refs_8_.refs_34_), channel_id=1, source_target_pairs={{0,1},{1,0},{2,3},{3,2},{4,5},{5,4},{6,7},{7,6},{8,9},{9,8},{10,11... | collective-permute-start | bytes 786440 | tf_op jit(solution)/shard_map/ppermute | solution.py:431
  32.1 17.8 %collective-permute-start.2 = (bf16[128,1024]{1,0:T(8,128)(2,1)S(1)}, bf16[128,1024]{1,0:T(8,128)(2,1)S(1)}, u32[]{:S(2)}, u32[]{:S(2)}) collective-permute-start(bf16[128,1024]{1,0:T(8,128)(2,1)S(1)} %collective-permute-done.1.refs_2_.refs_16_), channel_id=1, source_target_pairs={{0,4},{1,5},{4,8},{5,9},{8,12},{9,13},{12,14},{13,15},{14,10},{15,... | collective-permute-start | bytes 786440 | tf_op jit(solution)/shard_map/ppermute | solution.py:431
  33.8 18.4 %collective-permute-start.12 = (bf16[128,1024]{1,0:T(8,128)(2,1)S(1)}, bf16[128,1024]{1,0:T(8,128)(2,1)S(1)}, u32[]{:S(2)}, u32[]{:S(2)}) collective-permute-start(bf16[128,1024]{1,0:T(8,128)(2,1)S(1)} %collective-permute-done.11.refs_6_.refs_32_), channel_id=1, source_target_pairs={{0,4},{1,5},{4,8},{5,9},{8,12},{9,13},{12,14},{13,15},{14,10},{15,... | collective-permute-start | bytes 786440 | tf_op jit(solution)/shard_map/ppermute | solution.py:431
  35.3 16.9 %collective-permute-start.6 = (bf16[128,1024]{1,0:T(8,128)(2,1)S(1)}, bf16[128,1024]{1,0:T(8,128)(2,1)S(1)}, u32[]{:S(2)}, u32[]{:S(2)}) collective-permute-start(bf16[128,1024]{1,0:T(8,128)(2,1)S(1)} %collective-permute-done.5.refs_4_.refs_18_), channel_id=1, source_target_pairs={{0,2},{1,3},{4,0},{5,1},{8,4},{9,5},{12,8},{13,9},{14,12},{15,13},... | collective-permute-start | bytes 786440 | tf_op jit(solution)/shard_map/ppermute | solution.py:431
  40.7 12.1 %collective-permute-start.17 = (bf16[128,1024]{1,0:T(8,128)(2,1)S(1)}, bf16[128,1024]{1,0:T(8,128)(2,1)S(1)}, u32[]{:S(2)}, u32[]{:S(2)}) collective-permute-start(bf16[128,1024]{1,0:T(8,128)(2,1)S(1)} %collective-permute-done.16.refs_5_.refs_8_.refs_38_), channel_id=1, source_target_pairs={{0,1},{1,0},{2,3},{3,2},{4,5},{5,4},{6,7},{7,6},{8,9},{9,8},{10,11... | collective-permute-start | bytes 786440 | tf_op jit(solution)/shard_map/ppermute | solution.py:431
  41.4 1.6 copy-start
  49.4 8.8 %collective-permute-start.18 = (bf16[128,1024]{1,0:T(8,128)(2,1)S(1)}, bf16[128,1024]{1,0:T(8,128)(2,1)S(1)}, u32[]{:S(2)}, u32[]{:S(2)}) collective-permute-start(bf16[128,1024]{1,0:T(8,128)(2,1)S(1)} %collective-permute-done.16.refs_5_.refs_8_.refs_38_), channel_id=1, source_target_pairs={{0,2},{1,3},{4,0},{5,1},{8,4},{9,5},{12,8},{13,9},{14,12},{15,13},... | collective-permute-start | bytes 786440 | tf_op jit(solution)/shard_map/ppermute | solution.py:431
  50.0 8.4 %collective-permute-start.8 = (bf16[128,1024]{1,0:T(8,128)(2,1)S(1)}, bf16[128,1024]{1,0:T(8,128)(2,1)S(1)}, u32[]{:S(2)}, u32[]{:S(2)}) collective-permute-start(bf16[128,1024]{1,0:T(8,128)(2,1)S(1)} %collective-permute-done.2.refs_2_.refs_20_), channel_id=1, source_target_pairs={{0,4},{1,5},{4,8},{5,9},{8,12},{9,13},{12,14},{13,15},{14,10},{15,... | collective-permute-start | bytes 786440 | tf_op jit(solution)/shard_map/ppermute | solution.py:431
  52.1 9.4 %collective-permute-start.3 = (bf16[128,1024]{1,0:T(8,128)(2,1)S(1)}, bf16[128,1024]{1,0:T(8,128)(2,1)S(1)}, u32[]{:S(2)}, u32[]{:S(2)}) collective-permute-start(bf16[128,1024]{1,0:T(8,128)(2,1)S(1)} %collective-permute-done.2.refs_2_.refs_20_), channel_id=1, source_target_pairs={{0,1},{1,0},{2,3},{3,2},{4,5},{5,4},{6,7},{7,6},{8,9},{9,8},{10,11... | collective-permute-start | bytes 786440 | tf_op jit(solution)/shard_map/ppermute | solution.py:431
  52.2 9.3 %collective-permute-start.13 = (bf16[128,1024]{1,0:T(8,128)(2,1)S(1)}, bf16[128,1024]{1,0:T(8,128)(2,1)S(1)}, u32[]{:S(2)}, u32[]{:S(2)}) collective-permute-start(bf16[128,1024]{1,0:T(8,128)(2,1)S(1)} %collective-permute-done.12.refs_4_.refs_6_.refs_36_), channel_id=1, source_target_pairs={{0,1},{1,0},{2,3},{3,2},{4,5},{5,4},{6,7},{7,6},{8,9},{9,8},{10,11... | collective-permute-start | bytes 786440 | tf_op jit(solution)/shard_map/ppermute | solution.py:431
  52.7 8.9 %collective-permute-start.7 = (bf16[128,1024]{1,0:T(8,128)(2,1)S(1)}, bf16[128,1024]{1,0:T(8,128)(2,1)S(1)}, u32[]{:S(2)}, u32[]{:S(2)}) collective-permute-start(bf16[128,1024]{1,0:T(8,128)(2,1)S(1)} %collective-permute-done.6.refs_3_.refs_4_.refs_22_), channel_id=1, source_target_pairs={{0,1},{1,0},{2,3},{3,2},{4,5},{5,4},{6,7},{7,6},{8,9},{9,8},{10,11... | collective-permute-start | bytes 786440 | tf_op jit(solution)/shard_map/ppermute | solution.py:431
  58.2 4.7 %collective-permute-start.19 = (bf16[128,1024]{1,0:T(8,128)(2,1)S(1)}, bf16[128,1024]{1,0:T(8,128)(2,1)S(1)}, u32[]{:S(2)}, u32[]{:S(2)}) collective-permute-start(bf16[128,1024]{1,0:T(8,128)(2,1)S(1)} %collective-permute-done.18.refs_8_.refs_40_), channel_id=1, source_target_pairs={{0,1},{1,0},{2,3},{3,2},{4,5},{5,4},{6,7},{7,6},{8,9},{9,8},{10,11... | collective-permute-start | bytes 786440 | tf_op jit(solution)/shard_map/ppermute | solution.py:431
  58.4 4.5 collective-permute-start.9
  62.2 1.0 copy-start.2
  (2 other events, 1.9 us)
